TPU v7x, 256 devices: a whole 4x4x8 slice. The times are simulated.
256 devices in a mesh: chain: 4 (over y), row: 64 (over x, z, core).
Axes of the slice: x: 4, y: 4, z: 8, core: 2. Of those that a mesh axis runs over, the one named last changes fastest.
Arguments:
- right_side: float32 [131072, 128], P('row'), may hold values from -6 to 6
- factor: bfloat16 [131072, 1, 2048], P('row', None, 'chain'), may hold values from -0.125 to 0.125
- tile_scales: float32 [256, 1, 4], P('row', None, 'chain'), may hold values from 0.5 to 2
- diag_inverse: float32 [1, 512, 2048], P(None, None, 'chain'), may hold values from -0.25 to 0.25
Outputs:
- updated: float32 [131072, 128], P('row')
All inputs are finite; a program needn't handle non-finite values.
Results may differ from a plain program's by a relative error of at most 0.0031.
Values may be sent and summed in bfloat16 or wider, within the bound.
No kernel may reach another device: no remote copies, remote signals or barrier semaphores. Data moves between devices by JAX's collectives and lax.ppermute only.
A program may use at most 64 MiB of HBM per device.

v0:
```python
import jax
import jax.numpy as jnp
from jax import lax
from jax.sharding import PartitionSpec as P


def spread(value, axis, source):
    kept = jnp.where(lax.axis_index(axis) == source, value, 0).astype(value.dtype)
    return lax.psum(kept, axis)


def local(right_side, factor, tile_scales, diag_inverse):
    chain_index = lax.axis_index("chain")
    row_index = lax.axis_index("row")
    chain_count = lax.axis_size("chain")
    local_rows, rhs_count = right_side.shape
    rounds = factor.shape[1]
    block_size = factor.shape[2]
    tile_count = local_rows // block_size
    block_count = rounds * chain_count
    window = block_count * block_size
    row_ids = row_index * local_rows + jnp.arange(local_rows, dtype=jnp.int32)
    lead_chain = (chain_index == 0).astype(jnp.float32)
    zero = jnp.int32(0)

    def step(column, carry):
        carried, solved = carry
        round_index = column // chain_count
        owner_chain = column % chain_count
        block_start = column * block_size
        holder_row = block_start // local_rows
        offset = block_start % local_rows
        holder = row_index == holder_row
        own_rhs = lax.dynamic_slice(right_side, (offset, zero), (block_size, rhs_count))
        own_part = lax.dynamic_slice(carried, (offset, zero), (block_size, rhs_count))
        contrib = lead_chain * own_rhs - own_part
        inverse = lax.dynamic_index_in_dim(diag_inverse, round_index, 0, keepdims=False)
        residue = lax.psum(contrib, "chain")
        solved_now = jnp.dot(
            inverse, residue, precision=lax.Precision.HIGHEST, preferred_element_type=jnp.float32
        )
        solved_low = spread(solved_now.astype(jnp.bfloat16), "row", holder_row)

        def update(running):
            panel = lax.dynamic_index_in_dim(factor, round_index, 1, keepdims=False)
            product = jnp.dot(panel, solved_low, preferred_element_type=jnp.float32)
            tile_scale = lax.dynamic_index_in_dim(tile_scales, round_index, 1, keepdims=False)
            product = (
                product.reshape(tile_count, block_size, rhs_count) * tile_scale[:, :, None]
            ).reshape(local_rows, rhs_count)
            below = row_ids >= block_start + block_size
            return running + jnp.where(below[:, None], product, 0.0)

        def unchanged(running):
            return running

        carried = lax.cond(chain_index == owner_chain, update, unchanged, carried)
        store_mask = holder & (chain_index == owner_chain)
        previous = lax.dynamic_slice(solved, (offset, zero), (block_size, rhs_count))
        solved = lax.dynamic_update_slice(
            solved, jnp.where(store_mask, solved_now, previous), (offset, zero)
        )
        return (carried, solved)

    carried = jnp.zeros((local_rows, rhs_count), jnp.float32)
    solved = jnp.zeros((local_rows, rhs_count), jnp.float32)
    carried, solved = lax.fori_loop(0, block_count, step, (carried, solved))
    partial_out = jnp.where((row_ids < window)[:, None], solved, lead_chain * right_side - carried)
    return lax.psum(partial_out, "chain")


def solution(mesh):
    return jax.shard_map(
        local,
        mesh=mesh,
        in_specs=(
            P("row", None),
            P("row", None, "chain"),
            P("row", None, "chain"),
            P(None, None, "chain"),
        ),
        out_specs=P("row", None),
        check_vma=False,
    )
```

profile of v0, /device:TPU:2, one launch (start us, length us, event | category | flops | bytes accessed | tf_op | source)
XLA Modules:
  0.0 992.6 jit_solution(1642614647050685760)
XLA Ops:
  7.4 0.0 copy-start.1
  7.4 0.0 copy-start
  7.4 0.1 broadcast.16
  7.5 1.0 broadcast.16.clone.1
  8.5 0.0 copy-done.1
  8.5 0.5 copy-done
  9.0 918.6 %while.22 = (s32[]{:T(128)}, f32[2048,128]{1,0:T(8,128)S(1)}, f32[2048,128]{1,0:T(8,128)}, s32[]{:T(128)}, f32[]{:T(128)}, /*index=5*/f32[2048,128]{1,0:T(8,128)...) while((s32[]{:T(128)}, f32[2048,128]{1,0:T(8,128)S(1)}, ...), condition=%wide.region_5.6_spmd.clone, body=%wide.region_0.5_spmd.clone.sunk | while | flops 672337920 | bytes 14176989 | solution.py:67
  9.0 0.0 all-reduce.6.cloned.1.call-start
  9.0 1.7 dynamic-slice_subtract_fusion.2
  10.7 0.0 all-reduce.6.cloned.1.call-update
  10.7 0.0 all-reduce.8.cloned.1.call-start
  10.8 1.0 constant_dynamic-slice_fusion.2
  11.7 0.1 copy.15
  11.9 50.2 %all-reduce.6.cloned.1.call-done = f32[512,128]{1,0:T(8,128)} async-done(((f32[512,128]{1,0:T(8,128)}), f32[512,128]{1,0:T(8,128)}) %all-reduce.6.cloned.1.call-update) | async-done | bytes 262160 | tf_op jit(solution)/shard_map/while/body/eval_jaxpr/psum | solution.py:38
  62.1 2.9 convert_select_fusion.2
  65.0 0.1 copy.16
  65.1 0.0 all-reduce.8.cloned.1.call-update
  65.1 0.7 constant_dynamic-update-slice_fusion.2
  65.8 175.1 %all-reduce.8.cloned.1.call-done = bf16[512,128]{0,1:T(8,128)(2,1)} async-done(((bf16[512,128]{0,1:T(8,128)(2,1)}), bf16[512,128]{0,1:T(8,128)(2,1)}) %all-reduce.8.cloned.1.call-update) | async-done | bytes 131088 | tf_op jit(solution)/shard_map/while/body/eval_jaxpr/psum | solution.py:9
  240.9 2.8 conditional.3
  240.9 2.3 convolution_multiply_fusion
  243.3 0.5 fusion.2
  243.8 0.0 all-reduce.6.cloned.1.call-start
  243.8 1.7 dynamic-slice_subtract_fusion.2
  245.5 0.0 all-reduce.6.cloned.1.call-update
  245.5 0.0 all-reduce.8.cloned.1.call-start
  245.6 1.0 constant_dynamic-slice_fusion.2
  246.6 0.1 copy.15
  246.8 43.2 %all-reduce.6.cloned.1.call-done = f32[512,128]{1,0:T(8,128)} async-done(((f32[512,128]{1,0:T(8,128)}), f32[512,128]{1,0:T(8,128)}) %all-reduce.6.cloned.1.call-update) | async-done | bytes 262160 | tf_op jit(solution)/shard_map/while/body/eval_jaxpr/psum | solution.py:38
  290.0 2.9 convert_select_fusion.2
  292.9 0.1 copy.16
  293.0 0.0 all-reduce.8.cloned.1.call-update
  293.1 0.7 constant_dynamic-update-slice_fusion.2
  293.8 175.0 %all-reduce.8.cloned.1.call-done = bf16[512,128]{0,1:T(8,128)(2,1)} async-done(((bf16[512,128]{0,1:T(8,128)(2,1)}), bf16[512,128]{0,1:T(8,128)(2,1)}) %all-reduce.8.cloned.1.call-update) | async-done | bytes 131088 | tf_op jit(solution)/shard_map/while/body/eval_jaxpr/psum | solution.py:9
  468.7 0.0 all-reduce.6.cloned.1.call-start
  468.7 1.7 dynamic-slice_subtract_fusion.2
  470.4 0.0 all-reduce.6.cloned.1.call-update
  470.4 0.0 all-reduce.8.cloned.1.call-start
  470.5 1.0 constant_dynamic-slice_fusion.2
  471.5 0.1 copy.15
  471.7 46.8 %all-reduce.6.cloned.1.call-done = f32[512,128]{1,0:T(8,128)} async-done(((f32[512,128]{1,0:T(8,128)}), f32[512,128]{1,0:T(8,128)}) %all-reduce.6.cloned.1.call-update) | async-done | bytes 262160 | tf_op jit(solution)/shard_map/while/body/eval_jaxpr/psum | solution.py:38
  518.4 2.9 convert_select_fusion.2
  521.3 0.1 copy.16
  521.5 0.0 all-reduce.8.cloned.1.call-update
  521.5 0.7 constant_dynamic-update-slice_fusion.2
  522.2 175.0 %all-reduce.8.cloned.1.call-done = bf16[512,128]{0,1:T(8,128)(2,1)} async-done(((bf16[512,128]{0,1:T(8,128)(2,1)}), bf16[512,128]{0,1:T(8,128)(2,1)}) %all-reduce.8.cloned.1.call-update) | async-done | bytes 131088 | tf_op jit(solution)/shard_map/while/body/eval_jaxpr/psum | solution.py:9
  697.2 0.0 all-reduce.6.cloned.1.call-start
  697.2 1.7 dynamic-slice_subtract_fusion.2
  698.9 0.0 all-reduce.6.cloned.1.call-update
  698.9 0.0 all-reduce.8.cloned.1.call-start
  699.0 1.0 constant_dynamic-slice_fusion.2
  699.9 0.1 copy.15
  700.1 48.6 %all-reduce.6.cloned.1.call-done = f32[512,128]{1,0:T(8,128)} async-done(((f32[512,128]{1,0:T(8,128)}), f32[512,128]{1,0:T(8,128)}) %all-reduce.6.cloned.1.call-update) | async-done | bytes 262160 | tf_op jit(solution)/shard_map/while/body/eval_jaxpr/psum | solution.py:38
  748.7 2.9 convert_select_fusion.2
  751.6 0.1 copy.16
  751.7 0.0 all-reduce.8.cloned.1.call-update
  751.8 0.7 constant_dynamic-update-slice_fusion.2
  752.5 175.1 %all-reduce.8.cloned.1.call-done = bf16[512,128]{0,1:T(8,128)(2,1)} async-done(((bf16[512,128]{0,1:T(8,128)(2,1)}), bf16[512,128]{0,1:T(8,128)(2,1)}) %all-reduce.8.cloned.1.call-update) | async-done | bytes 131088 | tf_op jit(solution)/shard_map/while/body/eval_jaxpr/psum | solution.py:9
  927.6 0.0 all-reduce.4.cloned.1.call-start
  927.6 2.8 subtract_select_fusion
  930.4 0.0 all-reduce.4.cloned.1.call-update
  930.5 52.5 %all-reduce.4.cloned.1.call-done = f32[2048,128]{1,0:T(8,128)} async-done(((f32[2048,128]{1,0:T(8,128)}), f32[2048,128]{1,0:T(8,128)}) %all-reduce.4.cloned.1.call-update) | async-done | bytes 1048592 | tf_op jit(solution)/shard_map/psum | solution.py:69
  982.9 2.3 copy.32
  (13 shorter events, 0.2 us)
Async XLA Ops:
  7.4 1.1 copy-start.1
  7.4 1.6 copy-start
  9.0 53.1 %all-reduce.6.cloned.1.call-start = ((), (), s32[]{:S(2)}) async-start(), calls=%async_computation.1 | async-start | bytes 524288 | tf_op jit(solution)/shard_map/while/body/eval_jaxpr/psum | solution.py:38
  10.7 230.2 %all-reduce.8.cloned.1.call-start = ((), (), s32[]{:S(2)}) async-start(), calls=%async_computation.2 | async-start | bytes 262144 | tf_op jit(solution)/shard_map/while/body/eval_jaxpr/psum | solution.py:9
  243.8 46.2 %all-reduce.6.cloned.1.call-start = ((), (), s32[]{:S(2)}) async-start(), calls=%async_computation.1 | async-start | bytes 524288 | tf_op jit(solution)/shard_map/while/body/eval_jaxpr/psum | solution.py:38
  245.5 223.2 %all-reduce.8.cloned.1.call-start = ((), (), s32[]{:S(2)}) async-start(), calls=%async_computation.2 | async-start | bytes 262144 | tf_op jit(solution)/shard_map/while/body/eval_jaxpr/psum | solution.py:9
  468.7 49.7 %all-reduce.6.cloned.1.call-start = ((), (), s32[]{:S(2)}) async-start(), calls=%async_computation.1 | async-start | bytes 524288 | tf_op jit(solution)/shard_map/while/body/eval_jaxpr/psum | solution.py:38
  470.4 226.7 %all-reduce.8.cloned.1.call-start = ((), (), s32[]{:S(2)}) async-start(), calls=%async_computation.2 | async-start | bytes 262144 | tf_op jit(solution)/shard_map/while/body/eval_jaxpr/psum | solution.py:9
  697.2 51.5 %all-reduce.6.cloned.1.call-start = ((), (), s32[]{:S(2)}) async-start(), calls=%async_computation.1 | async-start | bytes 524288 | tf_op jit(solution)/shard_map/while/body/eval_jaxpr/psum | solution.py:38
  698.9 228.7 %all-reduce.8.cloned.1.call-start = ((), (), s32[]{:S(2)}) async-start(), calls=%async_computation.2 | async-start | bytes 262144 | tf_op jit(solution)/shard_map/while/body/eval_jaxpr/psum | solution.py:9
  927.6 55.3 %all-reduce.4.cloned.1.call-start = ((), (), s32[]{:S(2)}) async-start(), calls=%async_computation | async-start | bytes 2097152 | tf_op jit(solution)/shard_map/psum | solution.py:69
Sparse Core Ops, SparseCore 0:
  12.1 49.9 all-reduce.5
  65.5 175.3 all-reduce.7
  246.9 43.0 all-reduce.5
  293.3 175.3 all-reduce.7
  471.5 46.8 all-reduce.5
  521.8 175.3 all-reduce.7
  700.3 48.3 all-reduce.5
  752.2 175.3 all-reduce.7
Sparse Core Ops, SparseCore 1:
  930.6 52.3 all-reduce.3
where the time goes:
time: 993 us
  waiting for transfers between devices  942 us (95%)
  between operations  14.8 us (1%)
  matrix products  13.7 us (1%)
  local copies, waits for them, and re-layouts  11.7 us (1%)
  other arithmetic  10.2 us (1%)
    psum x4, waiting for transfers between devices, spread(): return lax.psum(kept, axis)  700 us
    psum x4, waiting for transfers between devices, step(): residue = lax.psum(contrib, 'chain')  189 us
    psum x1, waiting for transfers between devices, local(): return lax.psum(partial_out, 'chain')  52.5 us
  transfers between devices with their start and end apart: 9, of which 9 were waited for; matrix products, arithmetic and copies ran while one was open for 1% of the time, Pallas kernels for 0%

commit v1 on v0

v1 whole, which is shorter than its diff:
```python
import jax
import jax.numpy as jnp
from jax import lax
from jax.experimental import pallas as pl
from jax.experimental.pallas import tpu as pltpu
from jax.sharding import PartitionSpec as P


BF16 = jnp.bfloat16
F32 = jnp.float32
BLOCK = 512
RHS = 128
CHAINS = 4
ROWS = 64
CHUNKS = 4
KERNEL_VMEM = 12 * 1024 * 1024

TREE = {
    (0, 0): ((0, 7), (1, 0), (1, 7), (3, 0), (3, 7)),
    (2, 1): ((1, 1), (2, 0), (2, 2), (3, 1)),
    (1, 3): ((0, 3), (1, 4), (2, 3), (2, 4)),
    (2, 6): ((1, 6), (2, 5), (2, 7), (3, 6)),
    (0, 2): ((0, 1), (1, 2), (3, 2), (3, 3)),
    (0, 5): ((0, 4), (0, 6), (1, 5), (3, 4), (3, 5)),
}
CENTRES = tuple(TREE)
RELAY = (0, 2)
CORE_PAIRS = [[2 * i, 2 * i + 1] for i in range(ROWS // 2)]

VMEM = pl.BlockSpec(memory_space=pltpu.VMEM)
HBM = pl.BlockSpec(memory_space=pltpu.HBM)
COLUMN = pltpu.VMEM((BLOCK, RHS), F32)
LOW = pltpu.VMEM((BLOCK, RHS), BF16)


def row_of(chip, core=0):
    return chip[0] * 16 + chip[1] * 2 + core


def device_of(chain, chip, core=0):
    return chain * ROWS + row_of(chip, core)


def fan_out(tree):
    rounds = max((len(leaves) + 1) // 2 for leaves in tree.values())
    steps = [[] for _ in range(rounds)]
    for chip, leaves in tree.items():
        for i, leaf in enumerate(leaves):
            steps[i // 2].append((chip, i % 2, leaf))
    return steps


def on_chip(value):
    return pltpu.with_memory_space_constraint(value, pltpu.VMEM)


def call(body, outs, specs, *args, scratch=()):
    args = [
        pltpu.with_memory_space_constraint(a, s.memory_space) for a, s in zip(args, specs)
    ]
    single = not isinstance(outs, tuple)
    return pl.pallas_call(
        body,
        out_shape=outs,
        in_specs=specs,
        out_specs=VMEM if single else (VMEM,) * len(outs),
        scratch_shapes=scratch,
        compiler_params=pltpu.CompilerParams(vmem_limit_bytes=KERNEL_VMEM),
    )(*args)


def dot(a, b):
    return jnp.dot(a, b, preferred_element_type=F32)


def split(value):
    high = value.astype(BF16)
    return high, (value - high.astype(F32)).astype(BF16)


def product(high_ref, low_ref, value):
    high, low = split(value)
    return dot(high_ref[...], high) + dot(high_ref[...], low) + dot(low_ref[...], high)


def chain_index():
    return lax.axis_index("chain")


def is_head():
    return lax.axis_index("row") == 0


def block(i):
    return pl.ds(pl.multiple_of(i * BLOCK, BLOCK), BLOCK)


def own(ref):
    return ref[block(chain_index()), :]


def tile(scales, panel, i, solved_low):
    return scales[i : i + 1, :] * dot(panel[i * BLOCK : (i + 1) * BLOCK, :], solved_low)


def first(
    scales_in, rhs_in, inverse_in, panel_in, rhs, panel, high, low, scales, u1, u23, inverse, mine, numbers, sems
):
    chunk = BLOCK // CHUNKS
    parts = [pl.ds(i * chunk, chunk) for i in range(CHUNKS)]
    tiles = [pl.ds(i * BLOCK, BLOCK) for i in range(CHAINS)]
    here = block(chain_index())

    def copies(source, target, slices, at):
        return [
            pltpu.make_async_copy(source.at[rows], target.at[rows], sems.at[at + n])
            for n, rows in enumerate(slices)
        ]

    scale_load = pltpu.make_async_copy(scales_in, numbers, sems.at[0])
    own_load = pltpu.make_async_copy(rhs_in.at[here, :], mine, sems.at[1])
    inverse_loads = copies(inverse_in, inverse, parts, 2)
    panel_loads = copies(panel_in, panel, tiles, 2 + CHUNKS)
    rhs_load = pltpu.make_async_copy(rhs_in, rhs, sems.at[2 + CHUNKS + CHAINS])
    own_load.start()
    for load in inverse_loads:
        load.start()
    scale_load.start()
    for n in (1, 2, 3, 0):
        panel_loads[n].start()
    rhs_load.start()
    own_load.wait()
    value_high, value_low = split(mine[...])
    x = []
    for n, rows in enumerate(parts):
        inverse_loads[n].wait()
        high_part, low_part = split(inverse[rows, :])
        high[rows, :], low[rows, :] = high_part, low_part
        part = dot(high_part, value_high) + dot(high_part, value_low)
        x.append((part + dot(low_part, value_high)).astype(BF16))
    x = jnp.concatenate(x, axis=0)
    scale_load.wait()
    for n in range(CHAINS):
        scales[n : n + 1, :] = jnp.full((1, RHS), numbers[n], F32)
    panel_loads[1].wait()
    u1[...] = tile(scales, panel, 1, x)
    for n in (2, 3):
        panel_loads[n].wait()
        u23[(n - 2) * BLOCK : (n - 1) * BLOCK, :] = tile(scales, panel, n, x).astype(BF16)
    panel_loads[0].wait()
    rhs_load.wait()


def bridge(scales, high, low, panel, out):
    last = panel[3 * BLOCK :, :]
    product = dot(last, high[...]) + dot(last, low[...])
    out[...] = (scales[3:4, :1] * product).astype(BF16)


def second(scales, rhs, high, low, panel, m1, s1, solved, r2, r3):
    x = product(high, low, own(rhs) - m1[...]).astype(BF16)
    solved[...] = x
    for n, ref in ((2, r2), (3, r3)):
        rows = slice(n * BLOCK, (n + 1) * BLOCK)
        past = s1[(n - 2) * BLOCK : (n - 1) * BLOCK, :].astype(F32)
        ref[...] = rhs[rows, :] - past - tile(scales, panel, n, x)


def across(r2, r3, bridged, out):
    high, low = split(r2[...])
    out[...] = r3[...] - dot(bridged[...], high) - dot(bridged[...], low)


def third(rhs, high, low, m1, m2, relayed, solved):
    value = jnp.where(chain_index() == 2, m2[...], own(rhs) - m1[...])
    x = product(high, low, value).astype(BF16).astype(F32)
    keep = is_head() & (chain_index() < CHAINS - 1)
    solved[...] = (jnp.where(keep, x, 0.0) + relayed[...].astype(F32)).astype(BF16)


def fourth(high, low, ra, rb, rc, solved, xa, xb, xc, out):
    x = product(high, low, ra[...] + rb[...] + rc[...])
    for part in (solved, xa, xb, xc):
        x = x + part[...].astype(F32)
    out[...] = x.astype(BF16)


def update(scales, panel, x, kept, ahead2, ahead1, ahead3):
    for ref, shift in ((ahead2, 2), (ahead1, 1), (ahead3, 3), (kept, 0)):
        i = lax.rem(chain_index() + shift, CHAINS)
        ref[...] = (scales[pl.ds(i, 1), :] * dot(panel[block(i), :], x[...])).astype(ref.dtype)


def total(x, kept, a2, a1, a3, out):
    summed = kept[...] + a2[...].astype(F32) + a1[...].astype(F32) + a3[...].astype(F32)
    out[...] = jnp.where(is_head(), -x[...].astype(F32), summed).astype(BF16)


def finish(rhs, mine, b2, b1, b3, out, stage, sems):
    head = is_head()
    copies = []
    for n, (ref, shift) in enumerate(((mine, 0), (b2, 2), (b1, 1), (b3, 3))):
        i = lax.rem(chain_index() + CHAINS - shift, CHAINS)
        rows = block(i)
        stage[n] = jnp.where(head, 0.0, rhs[rows, :]) - ref[...].astype(F32)
        copy = pltpu.make_async_copy(stage.at[n], out.at[rows, :], sems.at[n])
        copy.start()
        copies.append(copy)
    for copy in copies:
        copy.wait()


def both_cores(value):
    return lax.all_gather(value, "row", axis_index_groups=CORE_PAIRS)[0]


def send(value, pairs):
    return lax.ppermute(value, ("chain", "row"), pairs)


def local(right_side, factor, tile_scales, diag_inverse):
    scales = tile_scales.reshape(CHAINS)
    panel = factor.reshape(factor.shape[0], factor.shape[2])
    inverse = diag_inverse[0]
    root = CENTRES[0]

    right, panel, high, low, scales, u1, u23 = call(
        first,
        (
            pltpu.VMEM(right_side.shape, F32),
            pltpu.VMEM(panel.shape, BF16),
            pltpu.VMEM((BLOCK, BLOCK), BF16),
            pltpu.VMEM((BLOCK, BLOCK), BF16),
            pltpu.VMEM((CHAINS, RHS), F32),
            COLUMN,
            pltpu.VMEM((2 * BLOCK, RHS), BF16),
        ),
        [HBM] * 4,
        scales, right_side, inverse, panel,
        scratch=[
            pltpu.VMEM((BLOCK, BLOCK), F32),
            pltpu.VMEM((BLOCK, RHS), F32),
            pltpu.SMEM((CHAINS,), F32),
            pltpu.SemaphoreType.DMA((3 + CHUNKS + CHAINS,)),
        ],
    )
    m1 = send(u1, [(device_of(0, root), device_of(1, root))])
    s1 = send(u23, [(device_of(0, root), device_of(1, root))])
    bridged = call(bridge, pltpu.VMEM((BLOCK, BLOCK), BF16), [VMEM] * 4, scales, high, low, panel)
    bridged = send(bridged, [(device_of(2, root), device_of(1, root))])
    solved, r2, r3 = call(
        second,
        (LOW, COLUMN, COLUMN),
        [VMEM] * 7,
        scales, right, high, low, panel, m1, s1,
    )
    m2 = send(r2, [(device_of(1, root), device_of(2, root))])
    relayed = send(solved, [(device_of(1, root), device_of(1, RELAY))])
    residue = both_cores(call(across, COLUMN, [VMEM] * 3, r2, r3, bridged))
    r = [
        send(residue, [(device_of(1, a, core), device_of(3, b)) for a, core, b in step])
        for step in fan_out({root: CENTRES})
    ]
    solved = call(third, LOW, [VMEM] * 6, right, high, low, m1, m2, relayed)
    solved = both_cores(solved)
    inside = [
        fan_out({root: CENTRES[1:]}),
        fan_out({RELAY: [c for c in CENTRES[1:] if c != RELAY]}),
        fan_out({root: CENTRES[1:]}),
    ]
    s = []
    for n in range(3):
        pairs = [
            (device_of(k, a, core), device_of(k, b))
            for k, steps in enumerate(inside)
            for a, core, b in (steps[n] if n < len(steps) else [])
        ]
        s.append(send(solved, pairs))
    x = call(fourth, LOW, [VMEM] * 9, high, low, *r, solved, *s)
    x = both_cores(x)
    got = [
        lax.ppermute(x, "row", [(row_of(a, core), row_of(b)) for a, core, b in pairs])
        for pairs in fan_out(TREE)
    ]
    x = both_cores(sum(got, x))

    kept, *ahead = call(update, (COLUMN, LOW, LOW, LOW), [VMEM] * 3, scales, panel, x)

    def ring(value, shift):
        pairs = [(j, (j + shift) % CHAINS) for j in range(CHAINS)]
        return lax.ppermute(value, "chain", pairs)

    arrived = [ring(a, s) for a, s in zip(ahead, (2, 1, 3))]
    mine = call(total, LOW, [VMEM] * 5, x, kept, *arrived)
    theirs = [ring(mine, s) for s in (2, 1, 3)]
    return pl.pallas_call(
        finish,
        out_shape=jax.ShapeDtypeStruct(right_side.shape, F32),
        in_specs=[VMEM] * 5,
        out_specs=HBM,
        scratch_shapes=[
            pltpu.VMEM((CHAINS, BLOCK, RHS), F32),
            pltpu.SemaphoreType.DMA((CHAINS,)),
        ],
        compiler_params=pltpu.CompilerParams(vmem_limit_bytes=KERNEL_VMEM),
    )(on_chip(right), on_chip(mine), *map(on_chip, theirs))


def solution(mesh):
    return jax.shard_map(
        local,
        mesh=mesh,
        in_specs=(
            P("row", None),
            P("row", None, "chain"),
            P("row", None, "chain"),
            P(None, None, "chain"),
        ),
        out_specs=P("row", None),
        check_vma=False,
    )
```

time: 993 us -> 72.6 us (0.07)
  the two profiles are of different devices: /device:TPU:2 before, /device:TPU:32 now
where the time goes in v1:
time: 72.6 us; the launch traced here: 72.2 us
  waiting for transfers between devices  29.4 us (40%)
  starting transfers between devices  25.4 us (35%)
  Pallas kernels  8.95 us (12%)
  blocking collectives  8.16 us (11%)
    ppermute x3, waiting for transfers between devices, local(): lax.ppermute(x, 'row', [(row_of(a, core), row_of(b)) for a, core, b in pa...  17.4 us
    ppermute x6, starting transfers between devices, ring(): return lax.ppermute(value, 'chain', pairs)  15.3 us
    ppermute x6, waiting for transfers between devices, ring(): return lax.ppermute(value, 'chain', pairs)  12 us
    all_gather x4, blocking collectives, both_cores(): return lax.all_gather(value, 'row', axis_index_groups=CORE_PAIRS)[0]  8.16 us
    pallas_call x8, Pallas kernels, call(): pl.pallas_call(body, out_shape=outs, in_specs=specs, out_specs=VMEM if si...  7.92 us
    ppermute x11, starting transfers between devices, send(): return lax.ppermute(value, ('chain', 'row'), pairs)  7.43 us
    ppermute x3, starting transfers between devices, local(): lax.ppermute(x, 'row', [(row_of(a, core), row_of(b)) for a, core, b in pa...  2.63 us
  transfers between devices with their start and end apart: 20, of which 6 were waited for; matrix products, arithmetic and copies ran while one was open for 0% of the time, Pallas kernels for 3%

profile of v1, /device:TPU:32, one launch (start us, length us, event | category | flops | bytes accessed | tf_op | source)
XLA Modules:
  0.0 72.2 jit_solution(4537468073481090055)
XLA Ops:
  0.0 3.3 %shard_map.46 = (f32[2048,128]{1,0:T(8,128)S(1)}, bf16[2048,512]{1,0:T(8,128)(2,1)S(1)}, bf16[512,512]{1,0:T(8,128)(2,1)S(1)}, bf16[512,512]{1,0:T(8,128)(2,1)S(...) custom-call(f32[4]{0:T(128)} %bitcast.5, f32[2048,128]{1,0:T(8,128)} %rhs_in.1, ...), custom_call_target="tpu_custom_call" | custom-call | tf_op jit(solution)/shard_map/pallas_call | solution.py:62
  3.3 0.7 shard_map.48
  4.0 0.7 collective-permute-start.2
  4.7 0.7 collective-permute-start
  5.4 0.7 collective-permute-start.1
  6.1 0.0 collective-permute-done.m1
  6.1 0.0 collective-permute-done.1.s1
  6.1 1.4 %shard_map.47 = (bf16[512,128]{1,0:T(8,128)(2,1)S(1)}, f32[512,128]{1,0:T(8,128)S(1)}, f32[512,128]{1,0:T(8,128)S(1)}) custom-call(f32[4,128]{1,0:T(4,128)S(1)} %get-tuple-element.22.scales, f32[2048,128]{1,0:T(8,128)S(1)} %get-tuple-element.19.rhs, bf16[512,512]{1,0:T(8,128)(2,1)S(1)} %get-tuple-element.20.high, ...), custom_call_target="tpu_custom_call" | custom-call | tf_op jit(solution)/shard_map/pallas_call | solution.py:62
  7.6 0.7 collective-permute-start.6
  8.3 0.7 collective-permute-start.7
  8.9 0.0 collective-permute-done.2.bridged
  9.0 0.4 shard_map.49
  9.4 2.2 %all-gather = f32[1024,128]{1,0:T(8,128)S(1)} all-gather(f32[512,128]{1,0:T(8,128)S(1)} %shard_map.49), channel_id=2, replica_groups={{0,1},{2,3},{4,5},{6,7},{8,9},{10,11},{12,13},{14,15},{16,17},{18,19},{..., dimensions={0}, use_global_device_ids=true | all-gather | bytes 786432 | tf_op jit(solution)/shard_map/all_gather | solution.py:214
  11.6 0.0 collective-permute-done.7.relayed
  11.6 0.0 collective-permute-done.6.m2
  11.6 0.6 shard_map.50
  12.2 2.0 %all-gather.1 = bf16[1024,128]{1,0:T(8,128)(2,1)S(1)} all-gather(bf16[512,128]{1,0:T(8,128)(2,1)S(1)} %shard_map.50), channel_id=3, replica_groups={{0,1},{2,3},{4,5},{6,7},{8,9},{10,11},{12,13},{14,15},{16,17},{18,19},{..., dimensions={0}, use_global_device_ids=true | all-gather | bytes 393216 | tf_op jit(solution)/shard_map/all_gather | solution.py:214
  14.2 0.7 collective-permute-start.8
  14.9 0.7 collective-permute-start.3
  15.6 0.7 collective-permute-start.4
  16.3 0.7 collective-permute-start.5
  17.0 0.7 collective-permute-start.9
  17.7 0.0 collective-permute-done.8.xa
  17.7 0.7 collective-permute-start.10
  18.3 0.0 collective-permute-done.9.xb
  18.3 0.0 collective-permute-done.10.xc
  18.4 0.0 collective-permute-done.3.ra
  18.4 0.0 collective-permute-done.4.rb
  18.4 0.0 collective-permute-done.5.rc
  18.4 0.6 shard_map.51
  19.0 2.0 %all-gather.2 = bf16[1024,128]{1,0:T(8,128)(2,1)S(1)} all-gather(bf16[512,128]{1,0:T(8,128)(2,1)S(1)} %shard_map.51), channel_id=4, replica_groups={{0,1},{2,3},{4,5},{6,7},{8,9},{10,11},{12,13},{14,15},{16,17},{18,19},{..., dimensions={0}, use_global_device_ids=true | all-gather | bytes 393216 | tf_op jit(solution)/shard_map/all_gather | solution.py:214
  21.0 0.7 collective-permute-start.13
  21.7 0.7 collective-permute-start.12
  22.4 1.3 %collective-permute-start.11 = (bf16[512,128]{1,0:T(8,128)(2,1)S(1)}, bf16[512,128]{1,0:T(8,128)(2,1)S(1)}, u32[]{:S(2)}, u32[]{:S(2)}) collective-permute-start(bf16[512,128]{1,0:T(8,128)(2,1)S(1)} %slice.22), channel_id=1, source_target_pairs={{0,14},{1,16},{34,18},{35,32},{22,6},{23,24},{44,28},{45,42},{4,2}... | collective-permute-start | bytes 393224 | tf_op jit(solution)/shard_map/ppermute | solution.py:282
  23.7 0.0 collective-permute-done.13
  23.7 0.0 collective-permute-done.12
  23.7 17.4 %collective-permute-done.11 = bf16[512,128]{1,0:T(8,128)(2,1)S(1)} collective-permute-done((bf16[512,128]{1,0:T(8,128)(2,1)S(1)}, bf16[512,128]{1,0:T(8,128)(2,1)S(1)}, u32[]{:S(2)}, u32[]{:S(2)}) %collective-permute-start.11) | collective-permute-done | bytes 131104 | tf_op jit(solution)/shard_map/ppermute | solution.py:282
  41.1 2.0 %all-gather.3 = bf16[1024,128]{1,0:T(8,128)(2,1)S(1)} all-gather(bf16[512,128]{1,0:T(8,128)(2,1)S(1)} %add_add_fusion), channel_id=5, replica_groups={{0,1},{2,3},{4,5},{6,7},{8,9},{10,11},{12,13},{14,15},{16,17},{18,19},{..., dimensions={0}, use_global_device_ids=true | all-gather | bytes 393216 | tf_op jit(solution)/shard_map/all_gather | solution.py:214
  43.1 0.7 shard_map.52
  43.8 6.3 %collective-permute-start.14 = (bf16[512,128]{1,0:T(8,128)(2,1)S(1)}, bf16[512,128]{1,0:T(8,128)(2,1)S(1)}, u32[]{:S(2)}, u32[]{:S(2)}) collective-permute-start(bf16[512,128]{1,0:T(8,128)(2,1)S(1)} %get-tuple-element.30), channel_id=1, source_target_pairs={{0,128},{64,192},{128,0},{192,64},{1,129},{65,193},{129,1},{193,65... | collective-permute-start | bytes 393224 | tf_op jit(solution)/shard_map/ppermute | solution.py:291
  50.1 4.9 %collective-permute-start.15 = (bf16[512,128]{1,0:T(8,128)(2,1)S(1)}, bf16[512,128]{1,0:T(8,128)(2,1)S(1)}, u32[]{:S(2)}, u32[]{:S(2)}) collective-permute-start(bf16[512,128]{1,0:T(8,128)(2,1)S(1)} %get-tuple-element.31), channel_id=1, source_target_pairs={{0,64},{64,128},{128,192},{192,0},{1,65},{65,129},{129,193},{193,1... | collective-permute-start | bytes 393224 | tf_op jit(solution)/shard_map/ppermute | solution.py:291
  55.0 0.0 collective-permute-start.16
  55.0 0.0 collective-permute-done.14.a2
  55.0 3.0 %collective-permute-done.15.a1 = bf16[512,128]{1,0:T(8,128)(2,1)S(1)} collective-permute-done((bf16[512,128]{1,0:T(8,128)(2,1)S(1)}, bf16[512,128]{1,0:T(8,128)(2,1)S(1)}, u32[]{:S(2)}, u32[]{:S(2)}) %collective-permute-start.15) | collective-permute-done | bytes 131104 | tf_op jit(solution)/shard_map/ppermute | solution.py:291
  58.0 3.3 %collective-permute-done.16.a3 = bf16[512,128]{1,0:T(8,128)(2,1)S(1)} collective-permute-done((bf16[512,128]{1,0:T(8,128)(2,1)S(1)}, bf16[512,128]{1,0:T(8,128)(2,1)S(1)}, u32[]{:S(2)}, u32[]{:S(2)}) %collective-permute-start.16) | collective-permute-done | bytes 131104 | tf_op jit(solution)/shard_map/ppermute | solution.py:291
  61.3 0.1 shard_map.53.mine
  61.4 1.0 %collective-permute-start.17 = (bf16[512,128]{1,0:T(8,128)(2,1)S(1)}, bf16[512,128]{1,0:T(8,128)(2,1)S(1)}, u32[]{:S(2)}, u32[]{:S(2)}) collective-permute-start(bf16[512,128]{1,0:T(8,128)(2,1)S(1)} %shard_map.53.mine), channel_id=1, source_target_pairs={{0,128},{64,192},{128,0},{192,64},{1,129},{65,193},{129,1},{193,65... | collective-permute-start | bytes 393224 | tf_op jit(solution)/shard_map/ppermute | solution.py:291
  62.4 2.6 %collective-permute-start.18 = (bf16[512,128]{1,0:T(8,128)(2,1)S(1)}, bf16[512,128]{1,0:T(8,128)(2,1)S(1)}, u32[]{:S(2)}, u32[]{:S(2)}) collective-permute-start(bf16[512,128]{1,0:T(8,128)(2,1)S(1)} %shard_map.53.mine), channel_id=1, source_target_pairs={{0,64},{64,128},{128,192},{192,0},{1,65},{65,129},{129,193},{193,1... | collective-permute-start | bytes 393224 | tf_op jit(solution)/shard_map/ppermute | solution.py:291
  65.0 0.6 collective-permute-start.19
  65.6 3.5 %collective-permute-done.17.b2 = bf16[512,128]{1,0:T(8,128)(2,1)S(1)} collective-permute-done((bf16[512,128]{1,0:T(8,128)(2,1)S(1)}, bf16[512,128]{1,0:T(8,128)(2,1)S(1)}, u32[]{:S(2)}, u32[]{:S(2)}) %collective-permute-start.17) | collective-permute-done | bytes 131104 | tf_op jit(solution)/shard_map/ppermute | solution.py:291
  69.1 1.4 %collective-permute-done.18.b1 = bf16[512,128]{1,0:T(8,128)(2,1)S(1)} collective-permute-done((bf16[512,128]{1,0:T(8,128)(2,1)S(1)}, bf16[512,128]{1,0:T(8,128)(2,1)S(1)}, u32[]{:S(2)}, u32[]{:S(2)}) %collective-permute-start.18) | collective-permute-done | bytes 131104 | tf_op jit(solution)/shard_map/ppermute | solution.py:291
  70.5 0.7 collective-permute-done.19.b3
  71.2 1.0 %shard_map.54 = f32[2048,128]{1,0:T(8,128)} custom-call(f32[2048,128]{1,0:T(8,128)S(1)} %get-tuple-element.19.rhs, bf16[512,128]{1,0:T(8,128)(2,1)S(1)} %shard_map.53.mine, bf16[512,128]{1,0:T(8,128)(2,1)S(1)} %collective-permute-done.17.b2, bf16[512,128]{1,0:T(8,128)(2,1)S(1)} %collective-permute-done.18.b1, bf16[512,128]{1,0:T(8,128)(2,1)S(1)} %collective-permute-done.19.b3), custom_call_target="tpu_custom_call" | custom-call | tf_op jit(solution)/shard_map/pallas_call | solution.py:296
  (5 shorter events, 0.1 us)
Async XLA Ops:
  4.0 4.9 %collective-permute-start.2 = (bf16[512,512]{1,0:T(8,128)(2,1)S(1)}, bf16[512,512]{1,0:T(8,128)(2,1)S(1)}, u32[]{:S(2)}, u32[]{:S(2)}) collective-permute-start(bf16[512,512]{1,0:T(8,128)(2,1)S(1)} %shard_map.48), channel_id=1, source_target_pairs={{128,64}} | collective-permute-start | bytes 1572872 | tf_op jit(solution)/shard_map/ppermute | solution.py:218
  4.7 1.4 %collective-permute-start = (f32[512,128]{1,0:T(8,128)S(1)}, f32[512,128]{1,0:T(8,128)S(1)}, u32[]{:S(2)}, u32[]{:S(2)}) collective-permute-start(f32[512,128]{1,0:T(8,128)S(1)} %get-tuple-element.24), channel_id=1, source_target_pairs={{0,64}} | collective-permute-start | bytes 786440 | tf_op jit(solution)/shard_map/ppermute | solution.py:218
  5.4 0.7 collective-permute-start.1
  7.6 4.0 %collective-permute-start.6 = (f32[512,128]{1,0:T(8,128)S(1)}, f32[512,128]{1,0:T(8,128)S(1)}, u32[]{:S(2)}, u32[]{:S(2)}) collective-permute-start(f32[512,128]{1,0:T(8,128)S(1)} %get-tuple-element.26.r2), channel_id=1, source_target_pairs={{64,128}} | collective-permute-start | bytes 786440 | tf_op jit(solution)/shard_map/ppermute | solution.py:218
  8.3 3.3 %collective-permute-start.7 = (bf16[512,128]{1,0:T(8,128)(2,1)S(1)}, bf16[512,128]{1,0:T(8,128)(2,1)S(1)}, u32[]{:S(2)}, u32[]{:S(2)}) collective-permute-start(bf16[512,128]{1,0:T(8,128)(2,1)S(1)} %get-tuple-element.28), channel_id=1, source_target_pairs={{64,68}} | collective-permute-start | bytes 393224 | tf_op jit(solution)/shard_map/ppermute | solution.py:218
  14.2 3.4 %collective-permute-start.8 = (bf16[512,128]{1,0:T(8,128)(2,1)S(1)}, bf16[512,128]{1,0:T(8,128)(2,1)S(1)}, u32[]{:S(2)}, u32[]{:S(2)}) collective-permute-start(bf16[512,128]{1,0:T(8,128)(2,1)S(1)} %slice.21.solved), channel_id=1, source_target_pairs={{0,34},{1,22},{68,98},{69,86},{128,162},{129,150}} | collective-permute-start | bytes 393224 | tf_op jit(solution)/shard_map/ppermute | solution.py:218
  14.9 3.4 %collective-permute-start.3 = (f32[512,128]{1,0:T(8,128)S(1)}, f32[512,128]{1,0:T(8,128)S(1)}, u32[]{:S(2)}, u32[]{:S(2)}) collective-permute-start(f32[512,128]{1,0:T(8,128)S(1)} %slice.20), channel_id=1, source_target_pairs={{64,192},{65,226}} | collective-permute-start | bytes 786440 | tf_op jit(solution)/shard_map/ppermute | solution.py:218
  15.6 2.8 %collective-permute-start.4 = (f32[512,128]{1,0:T(8,128)S(1)}, f32[512,128]{1,0:T(8,128)S(1)}, u32[]{:S(2)}, u32[]{:S(2)}) collective-permute-start(f32[512,128]{1,0:T(8,128)S(1)} %slice.20), channel_id=1, source_target_pairs={{64,214},{65,236}} | collective-permute-start | bytes 786440 | tf_op jit(solution)/shard_map/ppermute | solution.py:218
  16.3 2.1 %collective-permute-start.5 = (f32[512,128]{1,0:T(8,128)S(1)}, f32[512,128]{1,0:T(8,128)S(1)}, u32[]{:S(2)}, u32[]{:S(2)}) collective-permute-start(f32[512,128]{1,0:T(8,128)S(1)} %slice.20), channel_id=1, source_target_pairs={{64,196},{65,202}} | collective-permute-start | bytes 786440 | tf_op jit(solution)/shard_map/ppermute | solution.py:218
  17.0 1.4 %collective-permute-start.9 = (bf16[512,128]{1,0:T(8,128)(2,1)S(1)}, bf16[512,128]{1,0:T(8,128)(2,1)S(1)}, u32[]{:S(2)}, u32[]{:S(2)}) collective-permute-start(bf16[512,128]{1,0:T(8,128)(2,1)S(1)} %slice.21.solved), channel_id=1, source_target_pairs={{0,44},{1,4},{68,108},{69,74},{128,172},{129,132}} | collective-permute-start | bytes 393224 | tf_op jit(solution)/shard_map/ppermute | solution.py:218
  17.7 0.7 collective-permute-start.10
  21.0 2.7 %collective-permute-start.13 = (bf16[512,128]{1,0:T(8,128)(2,1)S(1)}, bf16[512,128]{1,0:T(8,128)(2,1)S(1)}, u32[]{:S(2)}, u32[]{:S(2)}) collective-permute-start(bf16[512,128]{1,0:T(8,128)(2,1)S(1)} %slice.22), channel_id=1, source_target_pairs={{0,62},{10,58},{64,126},{74,122},{128,190},{138,186},{192,254},{20... | collective-permute-start | bytes 393224 | tf_op jit(solution)/shard_map/ppermute | solution.py:282
  21.7 2.0 %collective-permute-start.12 = (bf16[512,128]{1,0:T(8,128)(2,1)S(1)}, bf16[512,128]{1,0:T(8,128)(2,1)S(1)}, u32[]{:S(2)}, u32[]{:S(2)}) collective-permute-start(bf16[512,128]{1,0:T(8,128)(2,1)S(1)} %slice.22), channel_id=1, source_target_pairs={{0,30},{1,48},{34,36},{35,50},{22,38},{23,40},{44,46},{45,60},{4,5... | collective-permute-start | bytes 393224 | tf_op jit(solution)/shard_map/ppermute | solution.py:282
  22.4 18.7 %collective-permute-start.11 = (bf16[512,128]{1,0:T(8,128)(2,1)S(1)}, bf16[512,128]{1,0:T(8,128)(2,1)S(1)}, u32[]{:S(2)}, u32[]{:S(2)}) collective-permute-start(bf16[512,128]{1,0:T(8,128)(2,1)S(1)} %slice.22), channel_id=1, source_target_pairs={{0,14},{1,16},{34,18},{35,32},{22,6},{23,24},{44,28},{45,42},{4,2}... | collective-permute-start | bytes 393224 | tf_op jit(solution)/shard_map/ppermute | solution.py:282
  43.8 11.2 %collective-permute-start.14 = (bf16[512,128]{1,0:T(8,128)(2,1)S(1)}, bf16[512,128]{1,0:T(8,128)(2,1)S(1)}, u32[]{:S(2)}, u32[]{:S(2)}) collective-permute-start(bf16[512,128]{1,0:T(8,128)(2,1)S(1)} %get-tuple-element.30), channel_id=1, source_target_pairs={{0,128},{64,192},{128,0},{192,64},{1,129},{65,193},{129,1},{193,65... | collective-permute-start | bytes 393224 | tf_op jit(solution)/shard_map/ppermute | solution.py:291
  50.1 7.9 %collective-permute-start.15 = (bf16[512,128]{1,0:T(8,128)(2,1)S(1)}, bf16[512,128]{1,0:T(8,128)(2,1)S(1)}, u32[]{:S(2)}, u32[]{:S(2)}) collective-permute-start(bf16[512,128]{1,0:T(8,128)(2,1)S(1)} %get-tuple-element.31), channel_id=1, source_target_pairs={{0,64},{64,128},{128,192},{192,0},{1,65},{65,129},{129,193},{193,1... | collective-permute-start | bytes 393224 | tf_op jit(solution)/shard_map/ppermute | solution.py:291
  55.0 6.3 %collective-permute-start.16 = (bf16[512,128]{1,0:T(8,128)(2,1)S(1)}, bf16[512,128]{1,0:T(8,128)(2,1)S(1)}, u32[]{:S(2)}, u32[]{:S(2)}) collective-permute-start(bf16[512,128]{1,0:T(8,128)(2,1)S(1)} %get-tuple-element.32), channel_id=1, source_target_pairs={{0,192},{64,0},{128,64},{192,128},{1,193},{65,1},{129,65},{193,129... | collective-permute-start | bytes 393224 | tf_op jit(solution)/shard_map/ppermute | solution.py:291
  61.4 7.7 %collective-permute-start.17 = (bf16[512,128]{1,0:T(8,128)(2,1)S(1)}, bf16[512,128]{1,0:T(8,128)(2,1)S(1)}, u32[]{:S(2)}, u32[]{:S(2)}) collective-permute-start(bf16[512,128]{1,0:T(8,128)(2,1)S(1)} %shard_map.53.mine), channel_id=1, source_target_pairs={{0,128},{64,192},{128,0},{192,64},{1,129},{65,193},{129,1},{193,65... | collective-permute-start | bytes 393224 | tf_op jit(solution)/shard_map/ppermute | solution.py:291
  62.4 8.1 %collective-permute-start.18 = (bf16[512,128]{1,0:T(8,128)(2,1)S(1)}, bf16[512,128]{1,0:T(8,128)(2,1)S(1)}, u32[]{:S(2)}, u32[]{:S(2)}) collective-permute-start(bf16[512,128]{1,0:T(8,128)(2,1)S(1)} %shard_map.53.mine), channel_id=1, source_target_pairs={{0,64},{64,128},{128,192},{192,0},{1,65},{65,129},{129,193},{193,1... | collective-permute-start | bytes 393224 | tf_op jit(solution)/shard_map/ppermute | solution.py:291
  65.0 6.2 %collective-permute-start.19 = (bf16[512,128]{1,0:T(8,128)(2,1)S(1)}, bf16[512,128]{1,0:T(8,128)(2,1)S(1)}, u32[]{:S(2)}, u32[]{:S(2)}) collective-permute-start(bf16[512,128]{1,0:T(8,128)(2,1)S(1)} %shard_map.53.mine), channel_id=1, source_target_pairs={{0,192},{64,0},{128,64},{192,128},{1,193},{65,1},{129,65},{193,129... | collective-permute-start | bytes 393224 | tf_op jit(solution)/shard_map/ppermute | solution.py:291

commit v2 on v1

v2 whole, which is shorter than its diff:
```python
import jax
import jax.numpy as jnp
from jax import lax
from jax.experimental import pallas as pl
from jax.experimental.pallas import tpu as pltpu
from jax.sharding import PartitionSpec as P


BF16 = jnp.bfloat16
F32 = jnp.float32
BLOCK = 512
RHS = 128
CHAINS = 4
ROWS = 64
CHIPS = (4, 8)
KERNEL_VMEM = 12 * 1024 * 1024

TREE = {
    (0, 0): ((0, 7), (1, 0), (1, 7), (3, 0), (3, 7)),
    (2, 1): ((1, 1), (2, 0), (2, 2), (3, 1)),
    (1, 3): ((0, 3), (1, 4), (2, 3), (2, 4)),
    (2, 6): ((1, 6), (2, 5), (2, 7), (3, 6)),
    (0, 2): ((0, 1), (1, 2), (3, 2), (3, 3)),
    (0, 5): ((0, 4), (0, 6), (1, 5), (3, 4), (3, 5)),
}
CENTRES = tuple(TREE)
RELAY = (1, 3)
CORE_PAIRS = [[2 * i, 2 * i + 1] for i in range(ROWS // 2)]

VMEM = pl.BlockSpec(memory_space=pltpu.VMEM)
HBM = pl.BlockSpec(memory_space=pltpu.HBM)
COLUMN = pltpu.VMEM((BLOCK, RHS), F32)
LOW = pltpu.VMEM((BLOCK, RHS), BF16)


def row_of(chip, core=0):
    return chip[0] * 16 + chip[1] * 2 + core


def device_of(chain, chip, core=0):
    return chain * ROWS + row_of(chip, core)


def hops(a, b):
    return sum(min((p - q) % n, (q - p) % n) for p, q, n in zip(a, b, CHIPS))


def fan_out(tree):
    rounds = max((len(leaves) + 1) // 2 for leaves in tree.values())
    steps = [[] for _ in range(rounds)]
    for chip, leaves in tree.items():
        for i, leaf in enumerate(sorted(leaves, key=lambda b: -hops(chip, b))):
            steps[i // 2].append((chip, i % 2, leaf))
    return steps


def on_chip(value):
    return pltpu.with_memory_space_constraint(value, pltpu.VMEM)


def call(body, outs, specs, *args, scratch=()):
    args = [
        pltpu.with_memory_space_constraint(a, s.memory_space) for a, s in zip(args, specs)
    ]
    single = not isinstance(outs, tuple)
    return pl.pallas_call(
        body,
        out_shape=outs,
        in_specs=specs,
        out_specs=VMEM if single else (VMEM,) * len(outs),
        scratch_shapes=scratch,
        compiler_params=pltpu.CompilerParams(vmem_limit_bytes=KERNEL_VMEM),
    )(*args)


def dot(a, b):
    return jnp.dot(a, b, preferred_element_type=F32)


def split(value):
    high = value.astype(BF16)
    return high, (value - high.astype(F32)).astype(BF16)


def wide(value):
    return jnp.concatenate(split(value), axis=1)


def product(halves, value):
    full = dot(halves[...], wide(value))
    return full[:BLOCK, :RHS] + full[:BLOCK, RHS:] + full[BLOCK:, :RHS] + full[BLOCK:, RHS:]


def chain_index():
    return lax.axis_index("chain")


def is_head():
    return lax.axis_index("row") == 0


def block(i):
    return pl.ds(pl.multiple_of(i * BLOCK, BLOCK), BLOCK)


def own(ref):
    return ref[block(chain_index()), :]


def tiles(scales, panel, start, solved_low):
    full = dot(panel[start * BLOCK :, :], solved_low)
    return [
        scales[i : i + 1, :] * full[(i - start) * BLOCK : (i - start + 1) * BLOCK, :]
        for i in range(start, CHAINS)
    ]


def first(
    scales_in, rhs_in, inverse_in, panel_in, rhs, panel, halves, scales, u, r1, inverse, mine, numbers, sems
):
    head, rest = pl.ds(0, BLOCK), pl.ds(BLOCK, 3 * BLOCK)
    loads = [
        pltpu.make_async_copy(source, target, sems.at[n])
        for n, (source, target) in enumerate(
            (
                (inverse_in, inverse),
                (rhs_in.at[block(chain_index()), :], mine),
                (scales_in, numbers),
                (panel_in.at[rest, :], panel.at[rest, :]),
                (panel_in.at[head, :], panel.at[head, :]),
                (rhs_in, rhs),
            )
        )
    ]
    for load in loads:
        load.start()
    loads[0].wait()
    halves[:BLOCK, :], halves[BLOCK:, :] = split(inverse[...])
    loads[1].wait()
    x = product(halves, mine[...]).astype(BF16)
    loads[2].wait()
    for n in range(CHAINS):
        scales[n : n + 1, :] = jnp.full((1, RHS), numbers[n], F32)
    loads[3].wait()
    for n, part in enumerate(tiles(scales, panel, 1, x)):
        u[n * BLOCK : (n + 1) * BLOCK, :] = part.astype(BF16)
        if n == 0:
            first_part = part
    for load in loads[4:]:
        load.wait()
    r1[...] = rhs[BLOCK : 2 * BLOCK, :] - first_part


def bridge(scales, halves, panel, out):
    last = panel[3 * BLOCK :, :]
    full = dot(last, halves[:BLOCK, :]) + dot(last, halves[BLOCK:, :])
    out[...] = (scales[3:4, :1] * full).astype(BF16)


def past(m1, n):
    return m1[(n - 1) * BLOCK : n * BLOCK, :].astype(F32)


def second(scales, rhs, halves, panel, m1, solved, r2):
    x = product(halves, own(rhs) - past(m1, 1)).astype(BF16)
    solved[...] = x
    part = scales[2:3, :] * dot(panel[2 * BLOCK : 3 * BLOCK, :], x)
    r2[...] = (rhs[2 * BLOCK : 3 * BLOCK, :] - past(m1, 2) - part).astype(r2.dtype)


def across(scales, rhs, panel, m1, solved, r2, bridged, out):
    part = scales[3:4, :] * dot(panel[3 * BLOCK :, :], solved[...])
    r3 = rhs[3 * BLOCK :, :] - past(m1, 3) - part
    full = dot(bridged[...], wide(r2[...]))
    out[...] = (r3 - full[:, :RHS] - full[:, RHS:]).astype(out.dtype)


def third(rhs, halves, m1, m2, relayed, solved):
    chain, row = chain_index(), lax.axis_index("row")
    value = jnp.where(chain == 2, m2[...], own(rhs) - past(m1, 1))
    relay = row == row_of(RELAY)
    x = product(halves, jnp.where(relay, relayed[...], value))
    keep = (is_head() & (chain < CHAINS - 1)) | (relay & (chain == 1))
    solved[...] = jnp.where(keep, x, 0.0).astype(BF16)


def fourth(halves, ra, rb, rc, solved, xa, xb, xc, out):
    x = product(halves, ra[...].astype(F32) + rb[...].astype(F32) + rc[...].astype(F32))
    for part in (solved, xa, xb, xc):
        x = x + part[...].astype(F32)
    out[...] = x.astype(BF16)


def update(scales, panel, x, ahead2, ahead1, ahead3, kept, full):
    full[...] = dot(panel[...], x[...])
    for ref, shift in ((ahead2, 2), (ahead1, 1), (ahead3, 3), (kept, 0)):
        i = lax.rem(chain_index() + shift, CHAINS)
        ref[...] = (scales[pl.ds(i, 1), :] * full[block(i), :]).astype(ref.dtype)


def total(x, kept, a1, a3, a2, out):
    summed = kept[...] + a2[...].astype(F32) + a1[...].astype(F32) + a3[...].astype(F32)
    out[...] = jnp.where(is_head(), -x[...].astype(F32), summed).astype(BF16)


def finish(rhs, mine, b1, b3, b2, out, stage, sems):
    head = is_head()
    copies = []
    for n, (ref, shift) in enumerate(((mine, 0), (b1, 1), (b3, 3), (b2, 2))):
        i = lax.rem(chain_index() + CHAINS - shift, CHAINS)
        rows = block(i)
        stage[n] = jnp.where(head, 0.0, rhs[rows, :]) - ref[...].astype(F32)
        copy = pltpu.make_async_copy(stage.at[n], out.at[rows, :], sems.at[n])
        copy.start()
        copies.append(copy)
    for copy in copies:
        copy.wait()


def both_cores(value):
    return lax.all_gather(value, "row", axis_index_groups=CORE_PAIRS)[0]


def send(value, pairs):
    return lax.ppermute(value, ("chain", "row"), pairs)


def local(right_side, factor, tile_scales, diag_inverse):
    scales = tile_scales.reshape(CHAINS)
    panel = factor.reshape(factor.shape[0], factor.shape[2])
    inverse = diag_inverse[0]
    root = CENTRES[0]

    right, panel, halves, scales, u, r1 = call(
        first,
        (
            pltpu.VMEM(right_side.shape, F32),
            pltpu.VMEM(panel.shape, BF16),
            pltpu.VMEM((2 * BLOCK, BLOCK), BF16),
            pltpu.VMEM((CHAINS, RHS), F32),
            pltpu.VMEM((3 * BLOCK, RHS), BF16),
            COLUMN,
        ),
        [HBM] * 4,
        scales, right_side, inverse, panel,
        scratch=[
            pltpu.VMEM((BLOCK, BLOCK), F32),
            pltpu.VMEM((BLOCK, RHS), F32),
            pltpu.SMEM((CHAINS,), F32),
            pltpu.SemaphoreType.DMA((6,)),
        ],
    )
    m1 = send(u, [(device_of(0, root), device_of(1, root))])
    bridged = call(
        bridge, pltpu.VMEM((BLOCK, BLOCK), BF16), [VMEM] * 3, scales, halves, panel
    )
    bridged = send(bridged, [(device_of(2, root), device_of(1, root))])
    relayed = send(r1, [(device_of(0, root), device_of(1, RELAY))])
    solved, r2 = call(
        second, (LOW, COLUMN), [VMEM] * 5, scales, right, halves, panel, m1
    )
    m2 = send(r2, [(device_of(1, root), device_of(2, root))])
    residue = call(across, LOW, [VMEM] * 7, scales, right, panel, m1, solved, r2, bridged)
    residue = both_cores(residue)
    r = [
        send(residue, [(device_of(1, a, core), device_of(3, b)) for a, core, b in step])
        for step in fan_out({root: CENTRES})
    ]
    solved = call(third, LOW, [VMEM] * 5, right, halves, m1, m2, relayed)
    solved = both_cores(solved)
    inside = [
        fan_out({root: CENTRES[1:]}),
        fan_out({RELAY: [c for c in CENTRES[1:] if c != RELAY]}),
        fan_out({root: CENTRES[1:]}),
    ]
    s = []
    for n in range(3):
        pairs = [
            (device_of(k, a, core), device_of(k, b))
            for k, steps in enumerate(inside)
            for a, core, b in (steps[n] if n < len(steps) else [])
        ]
        s.append(send(solved, pairs))
    x = call(fourth, LOW, [VMEM] * 8, halves, *r, solved, *s)
    x = both_cores(x)
    got = []
    for step in fan_out(TREE):
        pairs = [
            (device_of(k, a, core), device_of(k, b)) for k in range(CHAINS) for a, core, b in step
        ]
        got.append(send(x, pairs))
    x = both_cores(sum(got, x))

    ahead2, ahead1, ahead3, kept = call(
        update,
        (LOW, LOW, LOW, COLUMN),
        [VMEM] * 3,
        scales, panel, x,
        scratch=[pltpu.VMEM(panel.shape[:1] + (RHS,), F32)],
    )

    def ring(value, shift):
        pairs = [(j, (j + shift) % CHAINS) for j in range(CHAINS)]
        return lax.ppermute(value, "chain", pairs)

    arrived = [ring(a, s) for a, s in ((ahead1, 1), (ahead3, 3), (ahead2, 2))]
    mine = call(total, LOW, [VMEM] * 5, x, kept, *arrived)
    theirs = [ring(mine, s) for s in (1, 3, 2)]
    return pl.pallas_call(
        finish,
        out_shape=jax.ShapeDtypeStruct(right_side.shape, F32),
        in_specs=[VMEM] * 5,
        out_specs=HBM,
        scratch_shapes=[
            pltpu.VMEM((CHAINS, BLOCK, RHS), F32),
            pltpu.SemaphoreType.DMA((CHAINS,)),
        ],
        compiler_params=pltpu.CompilerParams(vmem_limit_bytes=KERNEL_VMEM),
    )(on_chip(right), on_chip(mine), *map(on_chip, theirs))


def solution(mesh):
    return jax.shard_map(
        local,
        mesh=mesh,
        in_specs=(
            P("row", None),
            P("row", None, "chain"),
            P("row", None, "chain"),
            P(None, None, "chain"),
        ),
        out_specs=P("row", None),
        check_vma=False,
    )
```

time: 72.6 us -> 63.3 us (0.87)
  the two profiles are of different devices: /device:TPU:32 before, /device:TPU:6 now
where the time goes in v2:
time: 63.3 us; the launch traced here: 63 us
  waiting for transfers between devices  28.3 us (45%)
  starting transfers between devices  18.4 us (29%)
  Pallas kernels  8 us (13%)
  blocking collectives  7.98 us (13%)
    ppermute x13, waiting for transfers between devices, send(): return lax.ppermute(value, ('chain', 'row'), pairs)  17 us
    ppermute x6, waiting for transfers between devices, ring(): return lax.ppermute(value, 'chain', pairs)  11.3 us
    ppermute x13, starting transfers between devices, send(): return lax.ppermute(value, ('chain', 'row'), pairs)  9.38 us
    ppermute x6, starting transfers between devices, ring(): return lax.ppermute(value, 'chain', pairs)  9.03 us
    all_gather x4, blocking collectives, both_cores(): return lax.all_gather(value, 'row', axis_index_groups=CORE_PAIRS)[0]  7.98 us
    pallas_call x8, Pallas kernels, call(): pl.pallas_call(body, out_shape=outs, in_specs=specs, out_specs=VMEM if si...  6.97 us
  transfers between devices with their start and end apart: 19, of which 7 were waited for; matrix products, arithmetic and copies ran while one was open for 0% of the time, Pallas kernels for 4%

profile of v2, /device:TPU:6, one launch (start us, length us, event | category | flops | bytes accessed | tf_op | source)
XLA Modules:
  0.0 63.0 jit_solution(4092488382038103635)
XLA Ops:
  0.0 3.0 %shard_map.46 = (f32[2048,128]{1,0:T(8,128)S(1)}, bf16[2048,512]{1,0:T(8,128)(2,1)S(1)}, bf16[1024,512]{1,0:T(8,128)(2,1)S(1)}, f32[4,128]{1,0:T(4,128)S(1)}, bf...) custom-call(f32[4]{0:T(128)} %bitcast.5, f32[2048,128]{1,0:T(8,128)} %rhs_in.1, f32[512,512]{1,0:T(8,128)} %bitcast.4, ...), custom_call_target="tpu_custom_call" | custom-call | tf_op jit(solution)/shard_map/pallas_call | solution.py:66
  3.0 0.7 %collective-permute-start = (bf16[1536,128]{1,0:T(8,128)(2,1)S(1)}, bf16[1536,128]{1,0:T(8,128)(2,1)S(1)}, u32[]{:S(2)}, u32[]{:S(2)}) collective-permute-start(bf16[1536,128]{1,0:T(8,128)(2,1)S(1)} %get-tuple-element.21), channel_id=1, source_target_pairs={{0,64}} | collective-permute-start | bytes 1179656 | tf_op jit(solution)/shard_map/ppermute | solution.py:225
  3.7 0.7 %shard_map.48 = bf16[512,512]{1,0:T(8,128)(2,1)S(1)} custom-call(f32[4,128]{1,0:T(4,128)S(1)} %get-tuple-element.19.scales, bf16[1024,512]{1,0:T(8,128)(2,1)S(1)} %get-tuple-element.18.halves, bf16[2048,512]{1,0:T(8,128)(2,1)S(1)} %get-tuple-element.20.panel), custom_call_target="tpu_custom_call" | custom-call | tf_op jit(solution)/shard_map/pallas_call | solution.py:66
  4.4 0.7 %collective-permute-start.1 = (bf16[512,512]{1,0:T(8,128)(2,1)S(1)}, bf16[512,512]{1,0:T(8,128)(2,1)S(1)}, u32[]{:S(2)}, u32[]{:S(2)}) collective-permute-start(bf16[512,512]{1,0:T(8,128)(2,1)S(1)} %shard_map.48), channel_id=1, source_target_pairs={{128,64}} | collective-permute-start | bytes 1572872 | tf_op jit(solution)/shard_map/ppermute | solution.py:225
  5.1 0.7 %collective-permute-start.6 = (f32[512,128]{1,0:T(8,128)S(1)}, f32[512,128]{1,0:T(8,128)S(1)}, u32[]{:S(2)}, u32[]{:S(2)}) collective-permute-start(f32[512,128]{1,0:T(8,128)S(1)} %get-tuple-element.24), channel_id=1, source_target_pairs={{0,86}} | collective-permute-start | bytes 786440 | tf_op jit(solution)/shard_map/ppermute | solution.py:225
  5.8 0.0 collective-permute-done.m1
  5.8 0.9 %shard_map.47 = (bf16[512,128]{1,0:T(8,128)(2,1)S(1)}, f32[512,128]{1,0:T(8,128)S(1)}) custom-call(f32[4,128]{1,0:T(4,128)S(1)} %get-tuple-element.19.scales, f32[2048,128]{1,0:T(8,128)S(1)} %get-tuple-element.17.rhs, bf16[1024,512]{1,0:T(8,128)(2,1)S(1)} %get-tuple-element.18.halves, bf16[2048,512]{1,0:T(8,128)(2,1)S(1)} %get-tuple-element.20.panel, ...), custom_call_target="tpu_custom_call" | custom-call | tf_op jit(solution)/shard_map/pallas_call | solution.py:66
  6.7 0.7 %collective-permute-start.5 = (f32[512,128]{1,0:T(8,128)S(1)}, f32[512,128]{1,0:T(8,128)S(1)}, u32[]{:S(2)}, u32[]{:S(2)}) collective-permute-start(f32[512,128]{1,0:T(8,128)S(1)} %get-tuple-element.23.r2), channel_id=1, source_target_pairs={{64,128}} | collective-permute-start | bytes 786440 | tf_op jit(solution)/shard_map/ppermute | solution.py:225
  7.4 0.0 collective-permute-done.1.bridged
  7.4 0.5 shard_map.49
  7.9 2.0 %all-gather = bf16[1024,128]{1,0:T(8,128)(2,1)S(1)} all-gather(bf16[512,128]{1,0:T(8,128)(2,1)S(1)} %shard_map.49), channel_id=2, replica_groups={{0,1},{2,3},{4,5},{6,7},{8,9},{10,11},{12,13},{14,15},{16,17},{18,19},{..., dimensions={0}, use_global_device_ids=true | all-gather | bytes 393216 | tf_op jit(solution)/shard_map/all_gather | solution.py:221
  9.9 0.7 %collective-permute-start.2 = (bf16[512,128]{1,0:T(8,128)(2,1)S(1)}, bf16[512,128]{1,0:T(8,128)(2,1)S(1)}, u32[]{:S(2)}, u32[]{:S(2)}) collective-permute-start(bf16[512,128]{1,0:T(8,128)(2,1)S(1)} %slice.20), channel_id=1, source_target_pairs={{64,214},{65,236}} | collective-permute-start | bytes 393224 | tf_op jit(solution)/shard_map/ppermute | solution.py:225
  10.6 0.7 %collective-permute-start.3 = (bf16[512,128]{1,0:T(8,128)(2,1)S(1)}, bf16[512,128]{1,0:T(8,128)(2,1)S(1)}, u32[]{:S(2)}, u32[]{:S(2)}) collective-permute-start(bf16[512,128]{1,0:T(8,128)(2,1)S(1)} %slice.20), channel_id=1, source_target_pairs={{64,226},{65,202}} | collective-permute-start | bytes 393224 | tf_op jit(solution)/shard_map/ppermute | solution.py:225
  11.2 0.7 %collective-permute-start.4 = (bf16[512,128]{1,0:T(8,128)(2,1)S(1)}, bf16[512,128]{1,0:T(8,128)(2,1)S(1)}, u32[]{:S(2)}, u32[]{:S(2)}) collective-permute-start(bf16[512,128]{1,0:T(8,128)(2,1)S(1)} %slice.20), channel_id=1, source_target_pairs={{64,196},{65,192}} | collective-permute-start | bytes 393224 | tf_op jit(solution)/shard_map/ppermute | solution.py:225
  11.9 0.0 collective-permute-done.6.relayed
  11.9 0.0 collective-permute-done.5.m2
  11.9 0.5 shard_map.50
  12.4 2.0 %all-gather.1 = bf16[1024,128]{1,0:T(8,128)(2,1)S(1)} all-gather(bf16[512,128]{1,0:T(8,128)(2,1)S(1)} %shard_map.50), channel_id=3, replica_groups={{0,1},{2,3},{4,5},{6,7},{8,9},{10,11},{12,13},{14,15},{16,17},{18,19},{..., dimensions={0}, use_global_device_ids=true | all-gather | bytes 393216 | tf_op jit(solution)/shard_map/all_gather | solution.py:221
  14.4 0.7 %collective-permute-start.7 = (bf16[512,128]{1,0:T(8,128)(2,1)S(1)}, bf16[512,128]{1,0:T(8,128)(2,1)S(1)}, u32[]{:S(2)}, u32[]{:S(2)}) collective-permute-start(bf16[512,128]{1,0:T(8,128)(2,1)S(1)} %slice.21.solved), channel_id=1, source_target_pairs={{0,22},{1,44},{86,108},{87,98},{128,150},{129,172}} | collective-permute-start | bytes 393224 | tf_op jit(solution)/shard_map/ppermute | solution.py:225
  15.1 0.7 %collective-permute-start.8 = (bf16[512,128]{1,0:T(8,128)(2,1)S(1)}, bf16[512,128]{1,0:T(8,128)(2,1)S(1)}, u32[]{:S(2)}, u32[]{:S(2)}) collective-permute-start(bf16[512,128]{1,0:T(8,128)(2,1)S(1)} %slice.21.solved), channel_id=1, source_target_pairs={{0,34},{1,10},{86,74},{87,68},{128,162},{129,138}} | collective-permute-start | bytes 393224 | tf_op jit(solution)/shard_map/ppermute | solution.py:225
  15.8 0.0 collective-permute-done.2.ra
  15.8 0.7 %collective-permute-start.9 = (bf16[512,128]{1,0:T(8,128)(2,1)S(1)}, bf16[512,128]{1,0:T(8,128)(2,1)S(1)}, u32[]{:S(2)}, u32[]{:S(2)}) collective-permute-start(bf16[512,128]{1,0:T(8,128)(2,1)S(1)} %slice.21.solved), channel_id=1, source_target_pairs={{0,4},{128,132}} | collective-permute-start | bytes 393224 | tf_op jit(solution)/shard_map/ppermute | solution.py:225
  16.5 0.0 collective-permute-done.3.rb
  16.5 0.0 collective-permute-done.4.rc
  16.5 0.0 collective-permute-done.7.xa
  16.5 0.0 collective-permute-done.8.xb
  16.5 0.0 collective-permute-done.9.xc
  16.5 0.5 shard_map.51
  17.0 2.0 %all-gather.2 = bf16[1024,128]{1,0:T(8,128)(2,1)S(1)} all-gather(bf16[512,128]{1,0:T(8,128)(2,1)S(1)} %shard_map.51), channel_id=4, replica_groups={{0,1},{2,3},{4,5},{6,7},{8,9},{10,11},{12,13},{14,15},{16,17},{18,19},{..., dimensions={0}, use_global_device_ids=true | all-gather | bytes 393216 | tf_op jit(solution)/shard_map/all_gather | solution.py:221
  19.0 0.7 %collective-permute-start.10 = (bf16[512,128]{1,0:T(8,128)(2,1)S(1)}, bf16[512,128]{1,0:T(8,128)(2,1)S(1)}, u32[]{:S(2)}, u32[]{:S(2)}) collective-permute-start(bf16[512,128]{1,0:T(8,128)(2,1)S(1)} %slice.22), channel_id=1, source_target_pairs={{0,30},{1,62},{34,18},{35,32},{22,40},{23,6},{44,28},{45,42},{4,54... | collective-permute-start | bytes 393224 | tf_op jit(solution)/shard_map/ppermute | solution.py:225
  19.7 0.7 %collective-permute-start.11 = (bf16[512,128]{1,0:T(8,128)(2,1)S(1)}, bf16[512,128]{1,0:T(8,128)(2,1)S(1)}, u32[]{:S(2)}, u32[]{:S(2)}) collective-permute-start(bf16[512,128]{1,0:T(8,128)(2,1)S(1)} %slice.22), channel_id=1, source_target_pairs={{0,14},{1,16},{34,36},{35,50},{22,24},{23,38},{44,46},{45,60},{4,2... | collective-permute-start | bytes 393224 | tf_op jit(solution)/shard_map/ppermute | solution.py:225
  20.4 1.3 %collective-permute-start.12 = (bf16[512,128]{1,0:T(8,128)(2,1)S(1)}, bf16[512,128]{1,0:T(8,128)(2,1)S(1)}, u32[]{:S(2)}, u32[]{:S(2)}) collective-permute-start(bf16[512,128]{1,0:T(8,128)(2,1)S(1)} %slice.22), channel_id=1, source_target_pairs={{0,48},{10,58},{64,112},{74,122},{128,176},{138,186},{192,240},{20... | collective-permute-start | bytes 393224 | tf_op jit(solution)/shard_map/ppermute | solution.py:225
  21.7 0.0 collective-permute-done.10
  21.7 0.0 collective-permute-done.11
  21.7 16.9 %collective-permute-done.12 = bf16[512,128]{1,0:T(8,128)(2,1)S(1)} collective-permute-done((bf16[512,128]{1,0:T(8,128)(2,1)S(1)}, bf16[512,128]{1,0:T(8,128)(2,1)S(1)}, u32[]{:S(2)}, u32[]{:S(2)}) %collective-permute-start.12) | collective-permute-done | bytes 131104 | tf_op jit(solution)/shard_map/ppermute | solution.py:225
  38.6 2.0 %all-gather.3 = bf16[1024,128]{1,0:T(8,128)(2,1)S(1)} all-gather(bf16[512,128]{1,0:T(8,128)(2,1)S(1)} %add_add_fusion), channel_id=5, replica_groups={{0,1},{2,3},{4,5},{6,7},{8,9},{10,11},{12,13},{14,15},{16,17},{18,19},{..., dimensions={0}, use_global_device_ids=true | all-gather | bytes 393216 | tf_op jit(solution)/shard_map/all_gather | solution.py:221
  40.7 0.9 %shard_map.52 = (bf16[512,128]{1,0:T(8,128)(2,1)S(1)}, bf16[512,128]{1,0:T(8,128)(2,1)S(1)}, bf16[512,128]{1,0:T(8,128)(2,1)S(1)}, f32[512,128]{1,0:T(8,128)S(1)}) custom-call(f32[4,128]{1,0:T(4,128)S(1)} %get-tuple-element.19.scales, bf16[2048,512]{1,0:T(8,128)(2,1)S(1)} %get-tuple-element.20.panel, bf16[512,128]{1,0:T(8,128)(2,1)S(1)} %slice.23.x), custom_call_target="tpu_custom_call" | custom-call | tf_op jit(solution)/shard_map/pallas_call | solution.py:66
  41.5 2.1 %collective-permute-start.13 = (bf16[512,128]{1,0:T(8,128)(2,1)S(1)}, bf16[512,128]{1,0:T(8,128)(2,1)S(1)}, u32[]{:S(2)}, u32[]{:S(2)}) collective-permute-start(bf16[512,128]{1,0:T(8,128)(2,1)S(1)} %get-tuple-element.26), channel_id=1, source_target_pairs={{0,64},{64,128},{128,192},{192,0},{1,65},{65,129},{129,193},{193,1... | collective-permute-start | bytes 393224 | tf_op jit(solution)/shard_map/ppermute | solution.py:304
  43.6 1.2 %collective-permute-start.14 = (bf16[512,128]{1,0:T(8,128)(2,1)S(1)}, bf16[512,128]{1,0:T(8,128)(2,1)S(1)}, u32[]{:S(2)}, u32[]{:S(2)}) collective-permute-start(bf16[512,128]{1,0:T(8,128)(2,1)S(1)} %get-tuple-element.27), channel_id=1, source_target_pairs={{0,192},{64,0},{128,64},{192,128},{1,193},{65,1},{129,65},{193,129... | collective-permute-start | bytes 393224 | tf_op jit(solution)/shard_map/ppermute | solution.py:304
  44.8 1.9 %collective-permute-start.15 = (bf16[512,128]{1,0:T(8,128)(2,1)S(1)}, bf16[512,128]{1,0:T(8,128)(2,1)S(1)}, u32[]{:S(2)}, u32[]{:S(2)}) collective-permute-start(bf16[512,128]{1,0:T(8,128)(2,1)S(1)} %get-tuple-element.28), channel_id=1, source_target_pairs={{0,128},{64,192},{128,0},{192,64},{1,129},{65,193},{129,1},{193,65... | collective-permute-start | bytes 393224 | tf_op jit(solution)/shard_map/ppermute | solution.py:304
  46.7 1.6 %collective-permute-done.13.a1 = bf16[512,128]{1,0:T(8,128)(2,1)S(1)} collective-permute-done((bf16[512,128]{1,0:T(8,128)(2,1)S(1)}, bf16[512,128]{1,0:T(8,128)(2,1)S(1)}, u32[]{:S(2)}, u32[]{:S(2)}) %collective-permute-start.13) | collective-permute-done | bytes 131104 | tf_op jit(solution)/shard_map/ppermute | solution.py:304
  48.3 1.6 %collective-permute-done.14.a3 = bf16[512,128]{1,0:T(8,128)(2,1)S(1)} collective-permute-done((bf16[512,128]{1,0:T(8,128)(2,1)S(1)}, bf16[512,128]{1,0:T(8,128)(2,1)S(1)}, u32[]{:S(2)}, u32[]{:S(2)}) %collective-permute-start.14) | collective-permute-done | bytes 131104 | tf_op jit(solution)/shard_map/ppermute | solution.py:304
  50.0 2.1 %collective-permute-done.15.a2 = bf16[512,128]{1,0:T(8,128)(2,1)S(1)} collective-permute-done((bf16[512,128]{1,0:T(8,128)(2,1)S(1)}, bf16[512,128]{1,0:T(8,128)(2,1)S(1)}, u32[]{:S(2)}, u32[]{:S(2)}) %collective-permute-start.15) | collective-permute-done | bytes 131104 | tf_op jit(solution)/shard_map/ppermute | solution.py:304
  52.1 0.1 shard_map.53.mine
  52.2 1.2 %collective-permute-start.16 = (bf16[512,128]{1,0:T(8,128)(2,1)S(1)}, bf16[512,128]{1,0:T(8,128)(2,1)S(1)}, u32[]{:S(2)}, u32[]{:S(2)}) collective-permute-start(bf16[512,128]{1,0:T(8,128)(2,1)S(1)} %shard_map.53.mine), channel_id=1, source_target_pairs={{0,64},{64,128},{128,192},{192,0},{1,65},{65,129},{129,193},{193,1... | collective-permute-start | bytes 393224 | tf_op jit(solution)/shard_map/ppermute | solution.py:304
  53.4 2.1 %collective-permute-start.17 = (bf16[512,128]{1,0:T(8,128)(2,1)S(1)}, bf16[512,128]{1,0:T(8,128)(2,1)S(1)}, u32[]{:S(2)}, u32[]{:S(2)}) collective-permute-start(bf16[512,128]{1,0:T(8,128)(2,1)S(1)} %shard_map.53.mine), channel_id=1, source_target_pairs={{0,192},{64,0},{128,64},{192,128},{1,193},{65,1},{129,65},{193,129... | collective-permute-start | bytes 393224 | tf_op jit(solution)/shard_map/ppermute | solution.py:304
  55.5 0.5 collective-permute-start.18
  56.0 2.4 %collective-permute-done.16.b1 = bf16[512,128]{1,0:T(8,128)(2,1)S(1)} collective-permute-done((bf16[512,128]{1,0:T(8,128)(2,1)S(1)}, bf16[512,128]{1,0:T(8,128)(2,1)S(1)}, u32[]{:S(2)}, u32[]{:S(2)}) %collective-permute-start.16) | collective-permute-done | bytes 131104 | tf_op jit(solution)/shard_map/ppermute | solution.py:304
  58.5 1.9 %collective-permute-done.17.b3 = bf16[512,128]{1,0:T(8,128)(2,1)S(1)} collective-permute-done((bf16[512,128]{1,0:T(8,128)(2,1)S(1)}, bf16[512,128]{1,0:T(8,128)(2,1)S(1)}, u32[]{:S(2)}, u32[]{:S(2)}) %collective-permute-start.17) | collective-permute-done | bytes 131104 | tf_op jit(solution)/shard_map/ppermute | solution.py:304
  60.3 1.6 %collective-permute-done.18.b2 = bf16[512,128]{1,0:T(8,128)(2,1)S(1)} collective-permute-done((bf16[512,128]{1,0:T(8,128)(2,1)S(1)}, bf16[512,128]{1,0:T(8,128)(2,1)S(1)}, u32[]{:S(2)}, u32[]{:S(2)}) %collective-permute-start.18) | collective-permute-done | bytes 131104 | tf_op jit(solution)/shard_map/ppermute | solution.py:304
  61.9 1.0 %shard_map.54 = f32[2048,128]{1,0:T(8,128)} custom-call(f32[2048,128]{1,0:T(8,128)S(1)} %get-tuple-element.17.rhs, bf16[512,128]{1,0:T(8,128)(2,1)S(1)} %shard_map.53.mine, bf16[512,128]{1,0:T(8,128)(2,1)S(1)} %collective-permute-done.16.b1, bf16[512,128]{1,0:T(8,128)(2,1)S(1)} %collective-permute-done.17.b3, bf16[512,128]{1,0:T(8,128)(2,1)S(1)} %collective-permute-done.18.b2), custom_call_target="tpu_custom_call" | custom-call | tf_op jit(solution)/shard_map/pallas_call | solution.py:309
  (5 shorter events, 0.1 us)
Async XLA Ops:
  3.0 2.8 %collective-permute-start = (bf16[1536,128]{1,0:T(8,128)(2,1)S(1)}, bf16[1536,128]{1,0:T(8,128)(2,1)S(1)}, u32[]{:S(2)}, u32[]{:S(2)}) collective-permute-start(bf16[1536,128]{1,0:T(8,128)(2,1)S(1)} %get-tuple-element.21), channel_id=1, source_target_pairs={{0,64}} | collective-permute-start | bytes 1179656 | tf_op jit(solution)/shard_map/ppermute | solution.py:225
  4.4 3.0 %collective-permute-start.1 = (bf16[512,512]{1,0:T(8,128)(2,1)S(1)}, bf16[512,512]{1,0:T(8,128)(2,1)S(1)}, u32[]{:S(2)}, u32[]{:S(2)}) collective-permute-start(bf16[512,512]{1,0:T(8,128)(2,1)S(1)} %shard_map.48), channel_id=1, source_target_pairs={{128,64}} | collective-permute-start | bytes 1572872 | tf_op jit(solution)/shard_map/ppermute | solution.py:225
  5.1 6.8 %collective-permute-start.6 = (f32[512,128]{1,0:T(8,128)S(1)}, f32[512,128]{1,0:T(8,128)S(1)}, u32[]{:S(2)}, u32[]{:S(2)}) collective-permute-start(f32[512,128]{1,0:T(8,128)S(1)} %get-tuple-element.24), channel_id=1, source_target_pairs={{0,86}} | collective-permute-start | bytes 786440 | tf_op jit(solution)/shard_map/ppermute | solution.py:225
  6.7 5.2 %collective-permute-start.5 = (f32[512,128]{1,0:T(8,128)S(1)}, f32[512,128]{1,0:T(8,128)S(1)}, u32[]{:S(2)}, u32[]{:S(2)}) collective-permute-start(f32[512,128]{1,0:T(8,128)S(1)} %get-tuple-element.23.r2), channel_id=1, source_target_pairs={{64,128}} | collective-permute-start | bytes 786440 | tf_op jit(solution)/shard_map/ppermute | solution.py:225
  9.9 5.9 %collective-permute-start.2 = (bf16[512,128]{1,0:T(8,128)(2,1)S(1)}, bf16[512,128]{1,0:T(8,128)(2,1)S(1)}, u32[]{:S(2)}, u32[]{:S(2)}) collective-permute-start(bf16[512,128]{1,0:T(8,128)(2,1)S(1)} %slice.20), channel_id=1, source_target_pairs={{64,214},{65,236}} | collective-permute-start | bytes 393224 | tf_op jit(solution)/shard_map/ppermute | solution.py:225
  10.6 5.9 %collective-permute-start.3 = (bf16[512,128]{1,0:T(8,128)(2,1)S(1)}, bf16[512,128]{1,0:T(8,128)(2,1)S(1)}, u32[]{:S(2)}, u32[]{:S(2)}) collective-permute-start(bf16[512,128]{1,0:T(8,128)(2,1)S(1)} %slice.20), channel_id=1, source_target_pairs={{64,226},{65,202}} | collective-permute-start | bytes 393224 | tf_op jit(solution)/shard_map/ppermute | solution.py:225
  11.2 5.3 %collective-permute-start.4 = (bf16[512,128]{1,0:T(8,128)(2,1)S(1)}, bf16[512,128]{1,0:T(8,128)(2,1)S(1)}, u32[]{:S(2)}, u32[]{:S(2)}) collective-permute-start(bf16[512,128]{1,0:T(8,128)(2,1)S(1)} %slice.20), channel_id=1, source_target_pairs={{64,196},{65,192}} | collective-permute-start | bytes 393224 | tf_op jit(solution)/shard_map/ppermute | solution.py:225
  14.4 2.1 %collective-permute-start.7 = (bf16[512,128]{1,0:T(8,128)(2,1)S(1)}, bf16[512,128]{1,0:T(8,128)(2,1)S(1)}, u32[]{:S(2)}, u32[]{:S(2)}) collective-permute-start(bf16[512,128]{1,0:T(8,128)(2,1)S(1)} %slice.21.solved), channel_id=1, source_target_pairs={{0,22},{1,44},{86,108},{87,98},{128,150},{129,172}} | collective-permute-start | bytes 393224 | tf_op jit(solution)/shard_map/ppermute | solution.py:225
  15.1 1.4 %collective-permute-start.8 = (bf16[512,128]{1,0:T(8,128)(2,1)S(1)}, bf16[512,128]{1,0:T(8,128)(2,1)S(1)}, u32[]{:S(2)}, u32[]{:S(2)}) collective-permute-start(bf16[512,128]{1,0:T(8,128)(2,1)S(1)} %slice.21.solved), channel_id=1, source_target_pairs={{0,34},{1,10},{86,74},{87,68},{128,162},{129,138}} | collective-permute-start | bytes 393224 | tf_op jit(solution)/shard_map/ppermute | solution.py:225
  15.8 0.7 %collective-permute-start.9 = (bf16[512,128]{1,0:T(8,128)(2,1)S(1)}, bf16[512,128]{1,0:T(8,128)(2,1)S(1)}, u32[]{:S(2)}, u32[]{:S(2)}) collective-permute-start(bf16[512,128]{1,0:T(8,128)(2,1)S(1)} %slice.21.solved), channel_id=1, source_target_pairs={{0,4},{128,132}} | collective-permute-start | bytes 393224 | tf_op jit(solution)/shard_map/ppermute | solution.py:225
  19.0 2.7 %collective-permute-start.10 = (bf16[512,128]{1,0:T(8,128)(2,1)S(1)}, bf16[512,128]{1,0:T(8,128)(2,1)S(1)}, u32[]{:S(2)}, u32[]{:S(2)}) collective-permute-start(bf16[512,128]{1,0:T(8,128)(2,1)S(1)} %slice.22), channel_id=1, source_target_pairs={{0,30},{1,62},{34,18},{35,32},{22,40},{23,6},{44,28},{45,42},{4,54... | collective-permute-start | bytes 393224 | tf_op jit(solution)/shard_map/ppermute | solution.py:225
  19.7 2.0 %collective-permute-start.11 = (bf16[512,128]{1,0:T(8,128)(2,1)S(1)}, bf16[512,128]{1,0:T(8,128)(2,1)S(1)}, u32[]{:S(2)}, u32[]{:S(2)}) collective-permute-start(bf16[512,128]{1,0:T(8,128)(2,1)S(1)} %slice.22), channel_id=1, source_target_pairs={{0,14},{1,16},{34,36},{35,50},{22,24},{23,38},{44,46},{45,60},{4,2... | collective-permute-start | bytes 393224 | tf_op jit(solution)/shard_map/ppermute | solution.py:225
  20.4 18.2 %collective-permute-start.12 = (bf16[512,128]{1,0:T(8,128)(2,1)S(1)}, bf16[512,128]{1,0:T(8,128)(2,1)S(1)}, u32[]{:S(2)}, u32[]{:S(2)}) collective-permute-start(bf16[512,128]{1,0:T(8,128)(2,1)S(1)} %slice.22), channel_id=1, source_target_pairs={{0,48},{10,58},{64,112},{74,122},{128,176},{138,186},{192,240},{20... | collective-permute-start | bytes 393224 | tf_op jit(solution)/shard_map/ppermute | solution.py:225
  41.5 6.8 %collective-permute-start.13 = (bf16[512,128]{1,0:T(8,128)(2,1)S(1)}, bf16[512,128]{1,0:T(8,128)(2,1)S(1)}, u32[]{:S(2)}, u32[]{:S(2)}) collective-permute-start(bf16[512,128]{1,0:T(8,128)(2,1)S(1)} %get-tuple-element.26), channel_id=1, source_target_pairs={{0,64},{64,128},{128,192},{192,0},{1,65},{65,129},{129,193},{193,1... | collective-permute-start | bytes 393224 | tf_op jit(solution)/shard_map/ppermute | solution.py:304
  43.6 6.4 %collective-permute-start.14 = (bf16[512,128]{1,0:T(8,128)(2,1)S(1)}, bf16[512,128]{1,0:T(8,128)(2,1)S(1)}, u32[]{:S(2)}, u32[]{:S(2)}) collective-permute-start(bf16[512,128]{1,0:T(8,128)(2,1)S(1)} %get-tuple-element.27), channel_id=1, source_target_pairs={{0,192},{64,0},{128,64},{192,128},{1,193},{65,1},{129,65},{193,129... | collective-permute-start | bytes 393224 | tf_op jit(solution)/shard_map/ppermute | solution.py:304
  44.8 7.2 %collective-permute-start.15 = (bf16[512,128]{1,0:T(8,128)(2,1)S(1)}, bf16[512,128]{1,0:T(8,128)(2,1)S(1)}, u32[]{:S(2)}, u32[]{:S(2)}) collective-permute-start(bf16[512,128]{1,0:T(8,128)(2,1)S(1)} %get-tuple-element.28), channel_id=1, source_target_pairs={{0,128},{64,192},{128,0},{192,64},{1,129},{65,193},{129,1},{193,65... | collective-permute-start | bytes 393224 | tf_op jit(solution)/shard_map/ppermute | solution.py:304
  52.2 6.3 %collective-permute-start.16 = (bf16[512,128]{1,0:T(8,128)(2,1)S(1)}, bf16[512,128]{1,0:T(8,128)(2,1)S(1)}, u32[]{:S(2)}, u32[]{:S(2)}) collective-permute-start(bf16[512,128]{1,0:T(8,128)(2,1)S(1)} %shard_map.53.mine), channel_id=1, source_target_pairs={{0,64},{64,128},{128,192},{192,0},{1,65},{65,129},{129,193},{193,1... | collective-permute-start | bytes 393224 | tf_op jit(solution)/shard_map/ppermute | solution.py:304
  53.4 6.9 %collective-permute-start.17 = (bf16[512,128]{1,0:T(8,128)(2,1)S(1)}, bf16[512,128]{1,0:T(8,128)(2,1)S(1)}, u32[]{:S(2)}, u32[]{:S(2)}) collective-permute-start(bf16[512,128]{1,0:T(8,128)(2,1)S(1)} %shard_map.53.mine), channel_id=1, source_target_pairs={{0,192},{64,0},{128,64},{192,128},{1,193},{65,1},{129,65},{193,129... | collective-permute-start | bytes 393224 | tf_op jit(solution)/shard_map/ppermute | solution.py:304
  55.5 6.5 %collective-permute-start.18 = (bf16[512,128]{1,0:T(8,128)(2,1)S(1)}, bf16[512,128]{1,0:T(8,128)(2,1)S(1)}, u32[]{:S(2)}, u32[]{:S(2)}) collective-permute-start(bf16[512,128]{1,0:T(8,128)(2,1)S(1)} %shard_map.53.mine), channel_id=1, source_target_pairs={{0,128},{64,192},{128,0},{192,64},{1,129},{65,193},{129,1},{193,65... | collective-permute-start | bytes 393224 | tf_op jit(solution)/shard_map/ppermute | solution.py:304
